TPU v7x, 256 devices: a whole 4x4x8 slice. The times are simulated.
256 devices in a mesh: dp: 8 (over z_hi, x), expert: 32 (over z_lo, y, core).
Axes of the slice: x: 4, y: 4, z: 8 (z_hi: 2, z_lo: 4; z = z_hi * 4 + z_lo), core: 2. Of those that a mesh axis runs over, the one named last changes fastest.
Arguments:
- tokens: bfloat16 [8192, 7168], P('expert', 'dp'), may hold values from -6 to 6
- cotangent: bfloat16 [8192, 7168], P('expert', 'dp'), may hold values from -6 to 6
- routing: int32 [8192, 8], P('expert'), may hold values from 0 to 255, as said below
- gate_values: float32 [8192, 8], P('expert'), may hold values from 0.05 to 0.6
- hidden_weight: bfloat16 [32, 7168, 2048], P('expert', 'dp'), may hold values from -0.0625 to 0.0625
- output_weight: bfloat16 [32, 1024, 7168], P('expert', None, 'dp'), may hold values from -0.1875 to 0.1875
Outputs:
- mixed: bfloat16 [8192, 7168], P('expert', 'dp')
- token_grad: bfloat16 [8192, 7168], P('expert', 'dp')
- hidden_grad: bfloat16 [32, 7168, 2048], P('expert', 'dp')
- output_grad: bfloat16 [32, 1024, 7168], P('expert', None, 'dp')
Inputs may be any that keep to these rules, and one draw needn't show every extreme that they name: `routing`: each row names 8 different experts. Within the 256 rows of one index of expert no expert is named by more than 16 rows, and in every such block some experts below 32 are named by exactly 16 rows.
All inputs are finite; a program needn't handle non-finite values.
Results may differ from a plain program's by a relative error of at most 0.022.
Values may be sent and summed in bfloat16 or wider, within the bound.
A program may use at most 64 MiB of HBM per device.

v0:
```python
import jax
import jax.numpy as jnp
from jax import lax
from jax.sharding import PartitionSpec as P

ROUTED = 256


def slot_table(routing_block, gate_block, expert_count, slot_count):
    tok_count = routing_block.shape[0]
    picked = routing_block.reshape(-1)
    onehot = (picked[:, None] == jnp.arange(expert_count, dtype=jnp.int32)[None, :]).astype(
        jnp.int32
    )
    earlier = jnp.cumsum(onehot, axis=0) - onehot
    ranking = jnp.sum(earlier * onehot, axis=1)
    slot_index = (picked * slot_count + ranking).reshape(tok_count, -1)
    target = jnp.arange(expert_count * slot_count, dtype=jnp.int32)
    matched = slot_index[None, :, :] == target[:, None, None]
    placed = jnp.any(matched, axis=2).astype(jnp.float32)
    gate_slot = jnp.sum(
        jnp.where(matched, gate_block[None, :, :], jnp.zeros_like(gate_block)[None, :, :]),
        axis=(1, 2),
    )
    return (placed, gate_slot)


def activate(hidden, half_width):
    gate_part = hidden[:, :half_width]
    up_part = hidden[:, half_width:]
    return (gate_part * jax.nn.sigmoid(gate_part) * up_part).astype(jnp.bfloat16)


def activate_grad(hidden, act_grad, half_width):
    gate_part = hidden[:, :half_width]
    up_part = hidden[:, half_width:]
    sigmoid_gate = jax.nn.sigmoid(gate_part)
    gate_grad = act_grad * up_part * sigmoid_gate * (1.0 + gate_part * (1.0 - sigmoid_gate))
    up_grad = act_grad * gate_part * sigmoid_gate
    return jnp.concatenate([gate_grad, up_grad], axis=1).astype(jnp.bfloat16)


def body(tokens, cotangent, routing, gate_values, hidden_weight, output_weight):
    tok_count, column_width = tokens.shape
    pick_count = routing.shape[1]
    expert_count = lax.axis_size("expert")
    slot_count = 2 * tok_count * pick_count // ROUTED
    row_total = expert_count * slot_count
    contract_cols = (((1,), (1,)), ((), ()))
    contract_rows = (((0,), (0,)), ((), ()))
    placed, gate_slot = slot_table(routing, gate_values, expert_count, slot_count)
    placed_half = placed.astype(jnp.bfloat16)
    send_shape = (expert_count, slot_count, column_width)
    token_rows = (
        jnp.dot(placed_half, tokens, preferred_element_type=jnp.float32)
        .astype(jnp.bfloat16)
        .reshape(send_shape)
    )
    cot_rows = (
        (gate_slot[:, None] * jnp.dot(placed_half, cotangent, preferred_element_type=jnp.float32))
        .astype(jnp.bfloat16)
        .reshape(send_shape)
    )
    inner_weight = hidden_weight[0]
    outer_weight = output_weight[0]
    half_width = outer_weight.shape[0]
    arrived = (
        lax.all_to_all(token_rows, "expert", split_axis=0, concat_axis=0, tiled=True),
        lax.all_to_all(cot_rows, "expert", split_axis=0, concat_axis=0, tiled=True),
    )
    expert_rows = arrived[0].reshape(row_total, column_width)
    scaled_cot = arrived[1].reshape(row_total, column_width)
    partial_hidden = jnp.dot(expert_rows, inner_weight, preferred_element_type=jnp.float32)
    hidden = lax.psum(partial_hidden.astype(jnp.bfloat16), "dp").astype(jnp.float32)
    active = activate(hidden, half_width)
    expert_out = jnp.dot(active, outer_weight, preferred_element_type=jnp.float32).astype(
        jnp.bfloat16
    )
    partial_act = lax.dot_general(
        scaled_cot, outer_weight, contract_cols, preferred_element_type=jnp.float32
    )
    act_grad = lax.psum(partial_act.astype(jnp.bfloat16), "dp").astype(jnp.float32)
    hidden_cot = activate_grad(hidden, act_grad, half_width)
    output_grad = lax.dot_general(
        active, scaled_cot, contract_rows, preferred_element_type=jnp.float32
    ).astype(jnp.bfloat16)
    hidden_grad = lax.dot_general(
        expert_rows, hidden_cot, contract_rows, preferred_element_type=jnp.float32
    ).astype(jnp.bfloat16)
    row_grad = lax.dot_general(
        hidden_cot, inner_weight, contract_cols, preferred_element_type=jnp.float32
    ).astype(jnp.bfloat16)
    returned = (
        lax.all_to_all(
            expert_out.reshape(send_shape), "expert", split_axis=0, concat_axis=0, tiled=True
        ),
        lax.all_to_all(
            row_grad.reshape(send_shape), "expert", split_axis=0, concat_axis=0, tiled=True
        ),
    )
    back_out = returned[0]
    back_grad = returned[1]
    back_out = back_out.reshape(row_total, column_width)
    back_grad = back_grad.reshape(row_total, column_width)
    weighted = placed * gate_slot[:, None]
    mixed = lax.dot_general(
        weighted,
        back_out.astype(jnp.float32),
        contract_rows,
        precision=lax.Precision.HIGHEST,
        preferred_element_type=jnp.float32,
    ).astype(jnp.bfloat16)
    token_grad = lax.dot_general(
        placed_half, back_grad, contract_rows, preferred_element_type=jnp.float32
    ).astype(jnp.bfloat16)
    return (mixed, token_grad, hidden_grad[None], output_grad[None])


def solution(mesh):
    return jax.shard_map(
        body,
        mesh=mesh,
        in_specs=(
            P("expert", "dp"),
            P("expert", "dp"),
            P("expert", None),
            P("expert", None),
            P("expert", "dp", None),
            P("expert", None, "dp"),
        ),
        out_specs=(
            P("expert", "dp"),
            P("expert", "dp"),
            P("expert", "dp", None),
            P("expert", None, "dp"),
        ),
        check_vma=False,
    )
```

profile of v0, /device:TPU:1, one launch (start us, length us, event | category | flops | bytes accessed | tf_op | source)
XLA Modules:
  0.0 334.4 jit_solution(6971142851061227383)
XLA Ops:
  8.4 9.1 %reduce-window.6 = s32[32,16,128]{2,1,0:T(8,128)S(1)} reduce-window(s32[32,16,128]{2,1,0:T(8,128)S(1)} %fusion.32, s32[]{:T(128)} %constant.6.clone.1), window={size=1x1x128 pad=0_0x0_0x127_0}, to_apply=%region_0.0 | reduce-window | flops 8323072 | bytes 524292 | tf_op jit(solution)/shard_map/reduce-window
  18.5 1.9 fusion
  20.5 1.3 select_reduce_fusion
  21.7 1.4 multiply_convert_fusion.1
  23.1 10.2 %all-to-all-start.2 = ((bf16[32,16,896]{2,1,0:T(8,128)(2,1)}), bf16[32,16,896]{2,1,0:T(8,128)(2,1)S(1)}, u32[]{:S(2)}, u32[]{:S(2)}) async-start(bf16[32,16,896]{2,1,0:T(8,128)(2,1)} %bitcast.65), calls=%async_computation.2 | async-start | bytes 1835008 | tf_op jit(solution)/shard_map/all_to_all | solution.py:69
  33.3 1.4 convolution_convert_fusion
  34.7 22.7 %all-to-all-done.2 = bf16[32,16,896]{2,1,0:T(8,128)(2,1)S(1)} async-done(((bf16[32,16,896]{2,1,0:T(8,128)(2,1)}), bf16[32,16,896]{2,1,0:T(8,128)(2,1)S(1)}, u32[]{:S(2)}, u32[]{:S(2)}) %all-to-all-start.2) | async-done | bytes 917536 | tf_op jit(solution)/shard_map/all_to_all | solution.py:69
  57.3 5.0 %all-to-all-start = ((bf16[32,16,896]{2,1,0:T(8,128)(2,1)}), bf16[32,16,896]{2,1,0:T(8,128)(2,1)}, u32[]{:S(2)}, u32[]{:S(2)}) async-start(bf16[32,16,896]{2,1,0:T(8,128)(2,1)} %bitcast.3), calls=%async_computation | async-start | bytes 1835008 | tf_op jit(solution)/shard_map/all_to_all | solution.py:68
  62.4 2.3 fusion.17
  64.7 21.8 %all-to-all-done = bf16[32,16,896]{2,1,0:T(8,128)(2,1)} async-done(((bf16[32,16,896]{2,1,0:T(8,128)(2,1)}), bf16[32,16,896]{2,1,0:T(8,128)(2,1)}, u32[]{:S(2)}, u32[]{:S(2)}) %all-to-all-start) | async-done | bytes 917536 | tf_op jit(solution)/shard_map/all_to_all | solution.py:68
  86.4 6.0 %fusion.5 = bf16[512,2048]{1,0:T(8,128)(2,1)} fusion(bf16[512,896]{1,0:T(8,128)(2,1)} %bitcast.4, bf16[1,896,2048]{2,1,0:T(8,128)(2,1)} %param.10), kind=kOutput, calls=%fused_computation.8 | convolution fusion | flops 1880096768 | bytes 6684672 | tf_op jit(solution)/shard_map/dot_general | solution.py:73
  92.4 160.4 %all-reduce.3.cloned.1.call-done = (bf16[512,2048]{1,0:T(8,128)(2,1)}, bf16[512,1024]{1,0:T(8,128)(2,1)}) async-done(((bf16[512,2048]{1,0:T(8,128)(2,1)}, bf16[512,1024]{1,0:T(8,128)(2,1)}), (bf16[512,2048]{1,0:T(8,128)(2,1)}, bf16[512,1024]{1,0:T(8,128)(2,1)})) %all-reduce.3.cloned.1.call-update) | async-done | bytes 3145744 | tf_op jit(solution)/shard_map/psum | solution.py:74
  252.9 2.2 convert_element_type.60
  255.1 2.3 fusion.10
  257.3 3.3 fusion.23
  260.6 10.7 %all-to-all-start.3 = ((bf16[32,16,896]{2,1,0:T(8,128)(2,1)}), bf16[32,16,896]{2,1,0:T(8,128)(2,1)}, u32[]{:S(2)}, u32[]{:S(2)}) async-start(bf16[32,16,896]{2,1,0:T(8,128)(2,1)} %bitcast.64), calls=%async_computation.3 | async-start | bytes 1835008 | tf_op jit(solution)/shard_map/all_to_all | solution.py:97
  271.3 3.4 %fusion.20 = bf16[512,896]{1,0:T(8,128)(2,1)} fusion(bf16[512,1024]{1,0:T(8,128)(2,1)} %get-tuple-element.8, bf16[1,1024,896]{2,1,0:T(8,128)(2,1)S(1)} %copy-done), kind=kOutput, calls=%fused_computation.26 | convolution fusion | flops 939982848 | bytes 3801088 | tf_op jit(solution)/shard_map/dot_general | solution.py:76
  274.7 20.7 %all-to-all-done.3 = bf16[32,16,896]{2,1,0:T(8,128)(2,1)} async-done(((bf16[32,16,896]{2,1,0:T(8,128)(2,1)}), bf16[32,16,896]{2,1,0:T(8,128)(2,1)}, u32[]{:S(2)}, u32[]{:S(2)}) %all-to-all-start.3) | async-done | bytes 917536 | tf_op jit(solution)/shard_map/all_to_all | solution.py:97
  295.4 5.0 %all-to-all-start.1 = ((bf16[32,16,896]{2,1,0:T(8,128)(2,1)}), bf16[32,16,896]{2,1,0:T(8,128)(2,1)}, u32[]{:S(2)}, u32[]{:S(2)}) async-start(bf16[32,16,896]{2,1,0:T(8,128)(2,1)} %bitcast.63), calls=%async_computation.1 | async-start | bytes 1835008 | tf_op jit(solution)/shard_map/all_to_all | solution.py:94
  300.4 4.1 %convert_bitcast_fusion.1 = bf16[1,1024,896]{2,1,0:T(8,128)(2,1)} fusion(bf16[512,1024]{1,0:T(8,128)(2,1)} %get-tuple-element.8, bf16[512,896]{1,0:T(8,128)(2,1)} %bitcast.62), kind=kOutput, calls=%fused_computation.23 | convolution fusion | flops 940441600 | bytes 3801088 | tf_op jit(solution)/shard_map/dot_general | solution.py:84
  304.5 5.1 %convert_bitcast_fusion = bf16[1,896,2048]{2,1,0:T(8,128)(2,1)} fusion(bf16[512,896]{1,0:T(8,128)(2,1)} %bitcast.4, bf16[512,1024]{1,0:T(8,128)(2,1)S(1)} %copy-done.2, bf16[512,1024]{1,0:T(8,128)(2,1)S(1)} %get-tuple-element.6), kind=kOutput, calls=%fused_computation.7 | convolution fusion | flops 1885077504 | bytes 6684672 | tf_op jit(solution)/shard_map/dot_general | solution.py:87
  309.6 2.4 convolution_convert_fusion.1
  312.1 12.5 %all-to-all-done.1 = bf16[32,16,896]{2,1,0:T(8,128)(2,1)} async-done(((bf16[32,16,896]{2,1,0:T(8,128)(2,1)}), bf16[32,16,896]{2,1,0:T(8,128)(2,1)}, u32[]{:S(2)}, u32[]{:S(2)}) %all-to-all-start.1) | async-done | bytes 917536 | tf_op jit(solution)/shard_map/all_to_all | solution.py:94
  324.5 3.1 convolution_convert_fusion.2
  (34 shorter events, 2.3 us)
Async XLA Ops:
  7.2 55.2 %copy-start = (bf16[1,1024,896]{2,1,0:T(8,128)(2,1)S(1)}, bf16[1,1024,896]{2,1,0:T(8,128)(2,1)}, u32[]{:S(2)}) copy-start(bf16[1,1024,896]{2,1,0:T(8,128)(2,1)} %param.11) | copy-start | bytes 5505028
  7.2 11.3 %copy-start.6 = (s32[256,8]{0,1:T(8,128)S(1)}, s32[256,8]{0,1:T(8,128)}, u32[]{:S(2)}) copy-start(s32[256,8]{0,1:T(8,128)} %param.8) | copy-start | bytes 24580
  7.2 13.3 %copy-start.7 = (f32[256,8]{0,1:T(8,128)S(1)}, f32[256,8]{0,1:T(8,128)}, u32[]{:S(2)}) copy-start(f32[256,8]{0,1:T(8,128)} %param.9) | copy-start | bytes 24580
  7.2 14.5 %copy-start.9 = (bf16[256,896]{1,0:T(8,128)(2,1)S(1)}, bf16[256,896]{1,0:T(8,128)(2,1)}, u32[]{:S(2)}) copy-start(bf16[256,896]{1,0:T(8,128)(2,1)} %param.7) | copy-start | bytes 1376260
  18.2 15.1 %copy-start.5 = (bf16[256,896]{1,0:T(8,128)(2,1)S(1)}, bf16[256,896]{1,0:T(8,128)(2,1)}, u32[]{:S(2)}) copy-start(bf16[256,896]{1,0:T(8,128)(2,1)} %param.6) | copy-start | bytes 1376260
  23.1 34.2 %all-to-all-start.2 = ((bf16[32,16,896]{2,1,0:T(8,128)(2,1)}), bf16[32,16,896]{2,1,0:T(8,128)(2,1)S(1)}, u32[]{:S(2)}, u32[]{:S(2)}) async-start(bf16[32,16,896]{2,1,0:T(8,128)(2,1)} %bitcast.65), calls=%async_computation.2 | async-start | bytes 1835008 | tf_op jit(solution)/shard_map/all_to_all | solution.py:69
  57.3 7.3 %copy-start.4 = (bf16[32,16,896]{2,1,0:T(8,128)(2,1)}, bf16[32,16,896]{2,1,0:T(8,128)(2,1)S(1)}, u32[]{:S(2)}) copy-start(bf16[32,16,896]{2,1,0:T(8,128)(2,1)S(1)} %all-to-all-done.2) | copy-start | bytes 2752516
  57.3 29.1 %all-to-all-start = ((bf16[32,16,896]{2,1,0:T(8,128)(2,1)}), bf16[32,16,896]{2,1,0:T(8,128)(2,1)}, u32[]{:S(2)}, u32[]{:S(2)}) async-start(bf16[32,16,896]{2,1,0:T(8,128)(2,1)} %bitcast.3), calls=%async_computation | async-start | bytes 1835008 | tf_op jit(solution)/shard_map/all_to_all | solution.py:68
  62.3 190.5 %all-reduce.3.cloned.1.call-start = ((), (), s32[]{:S(2)}) async-start(), calls=%async_computation.4 | async-start | bytes 6291456 | tf_op jit(solution)/shard_map/psum | solution.py:74
  252.9 2.2 copy-start.3
  255.1 2.3 copy-start.8
  257.3 3.3 copy-start.1
  260.6 34.8 %all-to-all-start.3 = ((bf16[32,16,896]{2,1,0:T(8,128)(2,1)}), bf16[32,16,896]{2,1,0:T(8,128)(2,1)}, u32[]{:S(2)}, u32[]{:S(2)}) async-start(bf16[32,16,896]{2,1,0:T(8,128)(2,1)} %bitcast.64), calls=%async_computation.3 | async-start | bytes 1835008 | tf_op jit(solution)/shard_map/all_to_all | solution.py:97
  295.4 29.1 %all-to-all-start.1 = ((bf16[32,16,896]{2,1,0:T(8,128)(2,1)}), bf16[32,16,896]{2,1,0:T(8,128)(2,1)}, u32[]{:S(2)}, u32[]{:S(2)}) async-start(bf16[32,16,896]{2,1,0:T(8,128)(2,1)} %bitcast.63), calls=%async_computation.1 | async-start | bytes 1835008 | tf_op jit(solution)/shard_map/all_to_all | solution.py:94
  300.4 4.1 %copy-start.2 = (bf16[512,1024]{1,0:T(8,128)(2,1)S(1)}, bf16[512,1024]{1,0:T(8,128)(2,1)}, u32[]{:S(2)}) copy-start(bf16[512,1024]{1,0:T(8,128)(2,1)} %copy-done.1) | copy-start | bytes 3145732
Sparse Core Ops, SparseCore 0:
  92.6 160.2 all-reduce.2
where the time goes:
time: 335 us; the launch traced here: 334 us
  waiting for transfers between devices  238 us (71%)
  matrix products  32.4 us (10%)
  starting transfers between devices  30.9 us (9%)
  other arithmetic  17.2 us (5%)
  between operations  14.2 us (4%)
    psum x1, waiting for transfers between devices, body(): lax.psum(partial_hidden.astype(jnp.bfloat16), 'dp').astype(jnp.float32)  160 us
    all_to_all x1, waiting for transfers between devices, body(): lax.all_to_all(cot_rows, 'expert', split_axis=0, concat_axis=0, tiled=True)  22.7 us
    all_to_all x1, waiting for transfers between devices, body(): lax.all_to_all(token_rows, 'expert', split_axis=0, concat_axis=0, tiled=T...  21.8 us
    all_to_all x1, waiting for transfers between devices, body(): lax.all_to_all(row_grad.reshape(send_shape), 'expert', split_axis=0, conc...  20.7 us
    all_to_all x1, waiting for transfers between devices, body(): lax.all_to_all(expert_out.reshape(send_shape), 'expert', split_axis=0, co...  12.5 us
    another operation x4, other arithmetic  11.7 us
    all_to_all x1, starting transfers between devices, body(): lax.all_to_all(row_grad.reshape(send_shape), 'expert', split_axis=0, conc...  10.7 us
    all_to_all x1, starting transfers between devices, body(): lax.all_to_all(cot_rows, 'expert', split_axis=0, concat_axis=0, tiled=True)  10.2 us
  transfers between devices with their start and end apart: 5, of which 5 were waited for; matrix products, arithmetic and copies ran while one was open for 6% of the time, Pallas kernels for 0%

commit v1 on v0

--- a/solution.py
+++ b/solution.py
@@ -1,9 +1,19 @@
+import functools
 import jax
 import jax.numpy as jnp
 from jax import lax
 from jax.sharding import PartitionSpec as P
 
 ROUTED = 256
+
+
+def mark_trails_by_axis(local_block, comm_axis):
+    current_block = lax.all_gather(local_block, comm_axis)
+    e_next = jnp.sum(current_block, 0)
+    return e_next
+
+
+raise_sample_over_axis = functools.partial(mark_trails_by_axis, comm_axis="dp")
 
 
 def slot_table(routing_block, gate_block, expert_count, slot_count):
@@ -71,7 +81,7 @@
     expert_rows = arrived[0].reshape(row_total, column_width)
     scaled_cot = arrived[1].reshape(row_total, column_width)
     partial_hidden = jnp.dot(expert_rows, inner_weight, preferred_element_type=jnp.float32)
-    hidden = lax.psum(partial_hidden.astype(jnp.bfloat16), "dp").astype(jnp.float32)
+    hidden = raise_sample_over_axis(partial_hidden.astype(jnp.bfloat16)).astype(jnp.float32)
     active = activate(hidden, half_width)
     expert_out = jnp.dot(active, outer_weight, preferred_element_type=jnp.float32).astype(
         jnp.bfloat16

time: 335 us -> 566 us (1.69)
  waiting for transfers between devices: 238 us -> 361 us
  blocking collectives: 0 us -> 108 us
  other arithmetic: 17.2 us -> 32.5 us
  starting transfers between devices: 30.9 us -> 15.9 us
    all_gather x0 -> x1, waiting for transfers between devices: none -> 236 us  [mark_trails_by_axis(): current_block = lax.all_gather(local_block, comm_axis)]
    all_to_all x0 -> x2, blocking collectives: none -> 108 us  [the longest x1 73.7 us: body(): lax.all_to_all(cot_rows, 'expert', split_axis=0, concat_axis=0, tiled=True)]
    psum x1, waiting for transfers between devices: 160 us -> 90.8 us  [body(): lax.psum(partial_act.astype(jnp.bfloat16), 'dp').astype(jnp.float32)]
    all_to_all x2 -> x0, waiting for transfers between devices: 44.4 us -> none  [the longest x1 22.7 us: body(): lax.all_to_all(cot_rows, 'expert', split_axis=0, concat_axis=0, tiled=True)]
    all_to_all x2 -> x0, starting transfers between devices: 15.2 us -> none  [the longest x1 10.2 us: body(): lax.all_to_all(cot_rows, 'expert', split_axis=0, concat_axis=0, tiled=True)]
    reduce_sum x0 -> x1, other arithmetic: none -> 10.8 us  [mark_trails_by_axis(): e_next = jnp.sum(current_block, 0)]
  transfers between devices with their start and end apart: 5 -> 4, of which waited for: 5 -> 4; matrix products, arithmetic and copies ran while one was open for 6% -> 6% of each run, Pallas kernels for 0% -> 0%
where the time goes in v1:
time: 566 us; the launch traced here: 565 us
  waiting for transfers between devices  361 us (64%)
  blocking collectives  108 us (19%)
  other arithmetic  32.5 us (6%)
  matrix products  29.2 us (5%)
  starting transfers between devices  15.9 us (3%)
  between operations  14.2 us (3%)
    all_gather x1, waiting for transfers between devices, mark_trails_by_axis(): current_block = lax.all_gather(local_block, comm_axis)  236 us
    psum x1, waiting for transfers between devices, body(): lax.psum(partial_act.astype(jnp.bfloat16), 'dp').astype(jnp.float32)  90.8 us
    all_to_all x1, blocking collectives, body(): lax.all_to_all(cot_rows, 'expert', split_axis=0, concat_axis=0, tiled=True)  73.7 us
    all_to_all x1, blocking collectives, body(): lax.all_to_all(token_rows, 'expert', split_axis=0, concat_axis=0, tiled=T...  34 us
    all_to_all x1, waiting for transfers between devices, body(): lax.all_to_all(row_grad.reshape(send_shape), 'expert', split_axis=0, conc...  20.7 us
    another operation x4, other arithmetic  14.4 us
    all_to_all x1, waiting for transfers between devices, body(): lax.all_to_all(expert_out.reshape(send_shape), 'expert', split_axis=0, co...  13.6 us
  transfers between devices with their start and end apart: 4, of which 4 were waited for; matrix products, arithmetic and copies ran while one was open for 6% of the time, Pallas kernels for 0%

profile of v1, /device:TPU:1, one launch (start us, length us, event | category | flops | bytes accessed | tf_op | source)
XLA Modules:
  0.0 565.0 jit_solution(16811683526052373065)
XLA Ops:
  7.2 1.0 copy.26
  8.5 9.1 %reduce-window.6 = s32[32,16,128]{2,1,0:T(8,128)S(1)} reduce-window(s32[32,16,128]{2,1,0:T(8,128)S(1)} %fusion.32, s32[]{:T(128)} %constant.5.clone.1), window={size=1x1x128 pad=0_0x0_0x127_0}, to_apply=%region_0.0 | reduce-window | flops 8323072 | bytes 524292 | tf_op jit(solution)/shard_map/reduce-window
  18.6 1.9 fusion
  20.9 34.0 %all_to_all.20 = bf16[32,16,896]{2,1,0:T(8,128)(2,1)S(1)} all-to-all(bf16[32,16,896]{2,1,0:T(8,128)(2,1)S(1)} %bitcast.62), channel_id=1, replica_groups=mesh['dp'=8,'expert'=32] {'expert'}, dimensions={0} | all-to-all | bytes 1835008 | tf_op jit(solution)/shard_map/all_to_all | solution.py:78
  55.0 1.0 copy-done.3
  55.9 5.7 %fusion.5 = bf16[512,2048]{1,0:T(8,128)(2,1)} fusion(bf16[512,896]{1,0:T(8,128)(2,1)S(1)} %bitcast.64, bf16[1,896,2048]{2,1,0:T(8,128)(2,1)} %param.10), kind=kOutput, calls=%fused_computation.8 | convolution fusion | flops 1880096768 | bytes 6684672 | tf_op jit(solution)/shard_map/dot_general | solution.py:83
  62.4 1.3 select_reduce_fusion
  64.1 73.7 %all_to_all.21 = bf16[32,16,896]{2,1,0:T(8,128)(2,1)S(1)} all-to-all(bf16[32,16,896]{2,1,0:T(8,128)(2,1)S(1)} %bitcast.70), channel_id=1, replica_groups=mesh['dp'=8,'expert'=32] {'expert'}, dimensions={0} | all-to-all | bytes 1835008 | tf_op jit(solution)/shard_map/all_to_all | solution.py:79
  138.8 2.3 fusion.17
  141.0 236.1 %all-gather.3.cloned.1.call-done = bf16[4096,2048]{1,0:T(8,128)(2,1)} async-done(((bf16[512,2048]{1,0:T(8,128)(2,1)}), bf16[4096,2048]{1,0:T(8,128)(2,1)}) %all-gather.3.cloned.1.call-update) | async-done | bytes 16777232 | tf_op jit(solution)/shard_map/all_gather | solution.py:11
  377.1 10.8 %reduce_sum.35 = bf16[512,2048]{1,0:T(8,128)(2,1)} reduce(bf16[8,512,2048]{2,1,0:T(8,128)(2,1)} %bitcast.61, bf16[]{:T(256)} %constant.16.clone.1), dimensions={0}, to_apply=%region_5.6 | reduce | flops 7340032 | bytes 18874370 | tf_op jit(solution)/shard_map/reduce_sum | solution.py:12
  387.9 4.0 convert_element_type.62
  391.9 90.8 %all-reduce.2.cloned.1.call-done = bf16[512,1024]{1,0:T(8,128)(2,1)} async-done(((bf16[512,1024]{1,0:T(8,128)(2,1)}), bf16[512,1024]{1,0:T(8,128)(2,1)}) %all-reduce.2.cloned.1.call-update) | async-done | bytes 1048592 | tf_op jit(solution)/shard_map/psum | solution.py:92
  482.8 4.9 fusion.10
  487.7 3.3 fusion.23
  491.0 10.8 %all-to-all-start.3 = ((bf16[32,16,896]{2,1,0:T(8,128)(2,1)}), bf16[32,16,896]{2,1,0:T(8,128)(2,1)}, u32[]{:S(2)}, u32[]{:S(2)}) async-start(bf16[32,16,896]{2,1,0:T(8,128)(2,1)} %bitcast.69), calls=%async_computation.3 | async-start | bytes 1835008 | tf_op jit(solution)/shard_map/all_to_all | solution.py:107
  501.9 3.4 fusion.20
  505.3 20.7 %all-to-all-done.3 = bf16[32,16,896]{2,1,0:T(8,128)(2,1)} async-done(((bf16[32,16,896]{2,1,0:T(8,128)(2,1)}), bf16[32,16,896]{2,1,0:T(8,128)(2,1)}, u32[]{:S(2)}, u32[]{:S(2)}) %all-to-all-start.3) | async-done | bytes 917536 | tf_op jit(solution)/shard_map/all_to_all | solution.py:107
  526.0 5.0 all-to-all-start.1
  531.0 4.2 convert_bitcast_fusion.1
  535.1 3.9 convert_bitcast_fusion
  539.1 2.4 convolution_convert_fusion.1
  541.5 13.6 %all-to-all-done.1 = bf16[32,16,896]{2,1,0:T(8,128)(2,1)} async-done(((bf16[32,16,896]{2,1,0:T(8,128)(2,1)}), bf16[32,16,896]{2,1,0:T(8,128)(2,1)}, u32[]{:S(2)}, u32[]{:S(2)}) %all-to-all-start.1) | async-done | bytes 917536 | tf_op jit(solution)/shard_map/all_to_all | solution.py:104
  555.1 3.1 convolution_convert_fusion.2
  (38 shorter events, 3.8 us)
Async XLA Ops:
  7.2 131.6 %copy-start = (bf16[1,1024,896]{2,1,0:T(8,128)(2,1)S(1)}, bf16[1,1024,896]{2,1,0:T(8,128)(2,1)}, u32[]{:S(2)}) copy-start(bf16[1,1024,896]{2,1,0:T(8,128)(2,1)} %param.11) | copy-start | bytes 5505028
  7.2 11.4 %copy-start.7 = (s32[256,8]{0,1:T(8,128)S(1)}, s32[256,8]{0,1:T(8,128)}, u32[]{:S(2)}) copy-start(s32[256,8]{0,1:T(8,128)} %param.8) | copy-start | bytes 24580
  7.2 13.3 %copy-start.6 = (bf16[256,896]{1,0:T(8,128)(2,1)S(1)}, bf16[256,896]{1,0:T(8,128)(2,1)}, u32[]{:S(2)}) copy-start(bf16[256,896]{1,0:T(8,128)(2,1)} %param.6) | copy-start | bytes 1376260
  7.2 369.9 %all-gather.3.cloned.1.call-start = ((), (), s32[]{:S(2)}) async-start(), calls=%async_computation.5 | async-start | bytes 18874368 | tf_op jit(solution)/shard_map/all_gather | solution.py:11
  55.0 1.0 copy-start.3
  61.7 0.7 copy-start.8
  61.7 2.0 copy-start.10
  61.7 421.1 %all-reduce.2.cloned.1.call-start = ((), (), s32[]{:S(2)}) async-start(), calls=%async_computation.4 | async-start | bytes 2097152 | tf_op jit(solution)/shard_map/psum | solution.py:92
  137.8 1.0 copy-start.5
  482.8 5.0 copy-start.9
  487.7 3.3 copy-start.1
  491.0 34.9 %all-to-all-start.3 = ((bf16[32,16,896]{2,1,0:T(8,128)(2,1)}), bf16[32,16,896]{2,1,0:T(8,128)(2,1)}, u32[]{:S(2)}, u32[]{:S(2)}) async-start(bf16[32,16,896]{2,1,0:T(8,128)(2,1)} %bitcast.69), calls=%async_computation.3 | async-start | bytes 1835008 | tf_op jit(solution)/shard_map/all_to_all | solution.py:107
  526.0 29.1 %all-to-all-start.1 = ((bf16[32,16,896]{2,1,0:T(8,128)(2,1)}), bf16[32,16,896]{2,1,0:T(8,128)(2,1)}, u32[]{:S(2)}, u32[]{:S(2)}) async-start(bf16[32,16,896]{2,1,0:T(8,128)(2,1)} %bitcast.68), calls=%async_computation.1 | async-start | bytes 1835008 | tf_op jit(solution)/shard_map/all_to_all | solution.py:104
  531.0 4.2 copy-start.2
  531.0 4.2 copy-start.4
Sparse Core Ops, SparseCore 0:
  61.8 315.2 all-gather.2
  380.3 102.4 all-reduce.1
